TPU v7x, 32 devices: a whole 2x2x4 slice. The times are simulated.
32 devices in a mesh: grp: 4 (over x, core), mem: 8 (over z, y).
Axes of the slice: x: 2, y: 2, z: 4, core: 2. Of those that a mesh axis runs over, the one named last changes fastest.
Arguments:
- embeddings: bfloat16 [16384, 768], P(('grp', 'mem')), may hold values from -1500 to 1500
- cluster_id: int32 [16384], P(('grp', 'mem')), may hold values from 0 to 3, as said below
- row_order: int32 [16384], P(('grp', 'mem')), may hold values from 0 to 16383, each once
- assignment: int32 [4], replicated, may hold values from 0 to 3, as said below
- placement: int32 [16384], P(('grp', 'mem')), may hold values from 0 to 7
Outputs:
- owner_best: float32 [32768], P(('grp', 'mem'))
Inputs may be any that keep to these rules, and one draw needn't show every extreme that they name: `cluster_id`: owner = assignment * 8 + placement; at most 32 rows of one device share an owner, and in every draw some owner gets exactly 32 rows from every device. `assignment`: each group owns exactly 1 cluster.
All inputs are finite; a program needn't handle non-finite values.
Results may differ from a plain program's by a relative error of at most 0.00034.
Values may be sent and summed in bfloat16 or wider, within the bound.
A program may use at most 128 MiB of HBM per device.

v0:
```python
import math

import jax
import jax.numpy as jnp
from jax import lax
from jax.sharding import PartitionSpec as P


def from_behind(block, axis, distance):
    devices = range(lax.axis_size(axis))
    route = [((i - distance) % len(devices), i) for i in devices]
    return lax.ppermute(block, axis, route)


def pair_tile(own_rows, piece_rows, with_columns):
    own_units, own_cluster, own_order = own_rows
    piece_units, piece_cluster, piece_order = piece_rows
    own_count = own_units.shape[0]
    block_rows = 512
    blocks = own_count // block_rows

    def block_max(packed):
        block_units, block_cluster, block_order = packed
        scores = jnp.einsum(
            "ik,jk->ij", block_units, piece_units, preferred_element_type=jnp.float32
        )
        same_cluster = (block_cluster[:, None] == piece_cluster[None, :]) & (
            block_cluster[:, None] >= 0
        )
        row_best = jnp.max(
            jnp.where(same_cluster & (piece_order[None, :] < block_order[:, None]), scores, -2.0),
            axis=1,
        )
        if with_columns:
            column_best = jnp.max(
                jnp.where(
                    same_cluster & (block_order[:, None] < piece_order[None, :]), scores, -2.0
                ),
                axis=0,
            )
            return (row_best, column_best)
        return row_best

    packed = (
        own_units.reshape(blocks, block_rows, own_units.shape[1]),
        own_cluster.reshape(blocks, block_rows),
        own_order.reshape(blocks, block_rows),
    )
    if with_columns:
        row_parts, column_parts = lax.map(block_max, packed)
        return (row_parts.reshape(own_count), jnp.max(column_parts, axis=0))
    return lax.map(block_max, packed).reshape(own_count)


def local(embeddings, cluster_id, row_order, assignment, placement):
    members = lax.axis_size("mem")
    groups = lax.axis_size("grp")
    owners = groups * members
    row_count = embeddings.shape[0]
    feature_count = embeddings.shape[1]
    capacity = max(2, 2 * row_count // owners)
    slot_count = owners * capacity
    widened = embeddings.astype(jnp.float32)
    unit_rows = (
        widened
        * lax.rsqrt(jnp.mean(widened * widened, axis=1, keepdims=True) + 1e-06)
        * (1.0 / math.sqrt(feature_count))
    ).astype(jnp.bfloat16)
    table_hits = cluster_id[:, None] == jnp.arange(assignment.shape[0], dtype=jnp.int32)[None, :]
    group_of = jnp.sum(jnp.where(table_hits, assignment[None, :], 0), axis=1)
    owner_id = group_of * members + placement
    owner_hits = (owner_id[:, None] == jnp.arange(owners, dtype=jnp.int32)[None, :]).astype(
        jnp.int32
    )
    rank_in_source = jnp.sum((jnp.cumsum(owner_hits, axis=0) - 1) * owner_hits, axis=1)
    target = owner_id * capacity + rank_in_source
    send_units = jnp.zeros((slot_count, feature_count), jnp.bfloat16).at[target].set(unit_rows)
    send_cluster = jnp.full((slot_count,), -1, jnp.int32).at[target].set(cluster_id)
    send_order = jnp.zeros((slot_count,), jnp.int32).at[target].set(row_order)
    got_units, got_cluster, got_order = (
        lax.all_to_all(send_units, ("grp", "mem"), split_axis=0, concat_axis=0, tiled=True),
        lax.all_to_all(send_cluster, ("grp", "mem"), split_axis=0, concat_axis=0, tiled=True),
        lax.all_to_all(send_order, ("grp", "mem"), split_axis=0, concat_axis=0, tiled=True),
    )
    own_rows = (got_units, got_cluster, got_order)
    half = members // 2
    start_best = pair_tile(own_rows, own_rows, False)

    def turn(step, carried):
        best_now, moving, column_acc = carried
        moving = from_behind((moving[0], moving[1], moving[2]), "mem", 1)
        column_acc = from_behind(column_acc, "mem", 1)
        row_best, column_best = pair_tile(own_rows, moving, True)
        column_acc = jnp.where(step < half, jnp.maximum(column_acc, column_best), column_acc)
        return (jnp.maximum(best_now, row_best), moving, column_acc)

    best, moving, column_acc = lax.fori_loop(
        1, half + 1, turn, (start_best, own_rows, jnp.full((slot_count,), -2.0, jnp.float32))
    )
    returned = from_behind(column_acc, "mem", half)
    best = jnp.maximum(best, returned)
    return jnp.maximum(best, -1.0)


def solution(mesh):
    return jax.shard_map(
        local,
        mesh=mesh,
        in_specs=(
            P(("grp", "mem"), None),
            P(("grp", "mem")),
            P(("grp", "mem")),
            P(),
            P(("grp", "mem")),
        ),
        out_specs=P(("grp", "mem")),
        check_vma=False,
    )
```

profile of v0, /device:TPU:0, one launch (start us, length us, event | category | flops | bytes accessed | tf_op | source)
XLA Modules:
  0.0 254.8 jit_solution(9089610358278299635)
XLA Ops:
  0.0 0.9 select_reduce_fusion.3
  0.9 0.7 multiply_add_fusion
  1.6 1.2 reduce-window.6
  2.7 0.2 slice_reduce_fusion
  3.0 0.1 fusion.16
  3.1 2.6 %scatter_custom_fusion.1 = s32[1024]{0:T(1024)S(1)} fusion(s32[512]{0:T(512)S(1)} %compare_select_fusion, s32[512]{0:T(512)} %param.13, s32[]{:T(128)} %constant.91.clone.1), kind=kCustom, calls=%fused_computation.44 | custom fusion | bytes 4608 | tf_op jit(solution)/shard_map/scatter | solution.py:79
  5.7 0.7 all_to_all.27
  6.4 7.3 %all-to-all-start.1 = ((s32[32,32,1]{1,2,0:T(1,128)}), s32[32,32,1]{1,2,0:T(1,128)S(1)}, u32[]{:S(2)}, u32[]{:S(2)}) async-start(s32[32,32,1]{1,2,0:T(1,128)} %all_to_all.27), calls=%async_computation.1 | async-start | bytes 32768 | tf_op jit(solution)/shard_map/all_to_all | solution.py:83
  13.7 1.4 fusion.7
  15.1 2.6 %scatter_custom_fusion = s32[1024]{0:T(1024)S(1)} fusion(s32[512]{0:T(512)S(1)} %compare_select_fusion, s32[512]{0:T(512)} %param.12, s32[]{:T(128)} %constant.96.clone.1), kind=kCustom, calls=%fused_computation.47 | custom fusion | bytes 4608 | tf_op jit(solution)/shard_map/scatter | solution.py:78
  17.7 0.7 all_to_all.24
  18.4 2.5 all-to-all-done.1
  20.9 3.4 %all-to-all-start = ((s32[32,32,1]{1,2,0:T(1,128)}), s32[32,32,1]{1,2,0:T(1,128)S(1)}, u32[]{:S(2)}, u32[]{:S(2)}) async-start(s32[32,32,1]{1,2,0:T(1,128)} %all_to_all.24), calls=%async_computation | async-start | bytes 32768 | tf_op jit(solution)/shard_map/all_to_all | solution.py:82
  24.3 3.9 %scatter_custom_fusion.2 = bf16[1024,768]{1,0:T(8,128)(2,1)} fusion(s32[512]{0:T(512)S(1)} %compare_select_fusion, bf16[512,768]{1,0:T(8,128)(2,1)S(1)} %copy-done, f32[]{:T(128)} %constant.100.clone.1, f32[512]{0:T(512)S(1)} %add_rsqrt_fusion, bf16[]{:T(256)} %constant.93.clone.1), kind=kCustom, calls=%fused_computation.27 | custom fusion | flops 1572864 | bytes 2361350 | tf_op jit(solution)/shard_map/scatter | solution.py:77
  28.2 3.2 %all-to-all-done = s32[32,32,1]{1,2,0:T(1,128)S(1)} async-done(((s32[32,32,1]{1,2,0:T(1,128)}), s32[32,32,1]{1,2,0:T(1,128)S(1)}, u32[]{:S(2)}, u32[]{:S(2)}) %all-to-all-start) | async-done | bytes 4128 | tf_op jit(solution)/shard_map/all_to_all | solution.py:82
  31.4 2.7 %all-to-all-start.2 = ((bf16[32,32,768]{2,1,0:T(8,128)(2,1)}), bf16[32,32,768]{2,1,0:T(8,128)(2,1)S(1)}, u32[]{:S(2)}, u32[]{:S(2)}) async-start(bf16[32,32,768]{2,1,0:T(8,128)(2,1)} %bitcast.11), calls=%async_computation.2 | async-start | bytes 3145728 | tf_op jit(solution)/shard_map/all_to_all | solution.py:81
  34.1 0.5 broadcast.110
  34.6 0.6 reduce.13
  35.3 0.1 all_to_all.29
  35.4 0.1 all_to_all.26
  35.5 0.6 reduce.12
  36.1 0.1 reshape.104
  36.2 0.1 reshape.105
  36.3 36.6 %all-to-all-done.2 = bf16[32,32,768]{2,1,0:T(8,128)(2,1)S(1)} async-done(((bf16[32,32,768]{2,1,0:T(8,128)(2,1)}), bf16[32,32,768]{2,1,0:T(8,128)(2,1)S(1)}, u32[]{:S(2)}, u32[]{:S(2)}) %all-to-all-start.2) | async-done | bytes 1572896 | tf_op jit(solution)/shard_map/all_to_all | solution.py:81
  72.9 1.2 copy.36
  74.0 2.7 %while.63 = (s32[]{:T(128)}, f32[2,512]{1,0:T(2,128)S(1)}, s32[2,512]{1,0:T(2,128)S(1)}, s32[1024]{0:T(1024)S(1)}, s32[1024]{0:T(1024)S(1)}, /*index=5*/s32[2,51...) while((s32[]{:T(128)}, f32[2,512]{1,0:T(2,128)S(1)}, ...), condition=%wide.region_10.11_spmd, body=%wide.region_8.10_spmd.sunk | while | flops 808452096 | bytes 2389105 | solution.py:52
  74.1 1.3 select_reduce_fusion.6
  75.4 1.3 select_reduce_fusion.6
  76.7 0.6 copy-done.1
  77.3 172.3 %while.65 = (s32[]{:T(128)}, f32[1024]{0:T(1024)S(1)}, bf16[1024,768]{1,0:T(8,128)(2,1)}, s32[1024]{0:T(1024)S(1)}, s32[1024]{0:T(1024)S(1)}, /*index=5*/f32[102...) while((s32[]{:T(128)}, f32[1024]{0:T(1024)S(1)}, ...), condition=%wide.wide.region_17.18_spmd.clone, body=%wide.wide.region_11.17_spmd.clone.sunk | while | flops 810553344 | bytes 11957810 | solution.py:97
  77.3 0.5 collective-permute-start.2
  77.8 0.5 collective-permute-start
  78.3 0.8 collective-permute-start.3
  79.1 37.3 %collective-permute-done = s32[1024]{0:T(1024)S(1)} collective-permute-done((s32[1024]{0:T(1024)S(1)}, s32[1024]{0:T(1024)S(1)}, u32[]{:S(2)}, u32[]{:S(2)}) %collective-permute-start) | collective-permute-done | bytes 4128 | tf_op jit(solution)/shard_map/while/body/eval_jaxpr/ppermute | solution.py:12
  116.4 4.1 %while.66 = (s32[]{:T(128)}, f32[2,512]{1,0:T(2,128)S(1)}, f32[2,1024]{1,0:T(2,128)S(1)}, s32[2,512]{1,0:T(2,128)S(1)}, s32[1024]{0:T(1024)S(1)}, /*index=5*/s32...) while((s32[]{:T(128)}, f32[2,512]{1,0:T(2,128)S(1)}, ...), condition=%wide.region_15.15_spmd, body=%wide.region_12.14_spmd.sunk | while | flops 810548224 | bytes 2401405 | solution.py:50
  116.4 1.9 select_reduce_fusion.7
  118.5 1.9 select_reduce_fusion.7
  120.6 1.2 copy.48
  121.8 0.3 collective-permute-start
  122.1 0.1 collective-permute-start.1
  122.1 0.1 collective-permute-start.3
  122.2 37.7 %collective-permute-done = s32[1024]{0:T(1024)S(1)} collective-permute-done((s32[1024]{0:T(1024)S(1)}, s32[1024]{0:T(1024)S(1)}, u32[]{:S(2)}, u32[]{:S(2)}) %collective-permute-start) | collective-permute-done | bytes 4128 | tf_op jit(solution)/shard_map/while/body/eval_jaxpr/ppermute | solution.py:12
  160.0 4.1 %while.66 = (s32[]{:T(128)}, f32[2,512]{1,0:T(2,128)S(1)}, f32[2,1024]{1,0:T(2,128)S(1)}, s32[2,512]{1,0:T(2,128)S(1)}, s32[1024]{0:T(1024)S(1)}, /*index=5*/s32...) while((s32[]{:T(128)}, f32[2,512]{1,0:T(2,128)S(1)}, ...), condition=%wide.region_15.15_spmd, body=%wide.region_12.14_spmd.sunk | while | flops 810548224 | bytes 2401405 | solution.py:50
  160.0 1.9 select_reduce_fusion.7
  162.1 1.9 select_reduce_fusion.7
  164.2 1.2 copy.48
  165.3 0.1 collective-permute-start
  165.4 0.1 collective-permute-start.1
  165.5 0.1 collective-permute-start.3
  165.6 37.0 %collective-permute-done = s32[1024]{0:T(1024)S(1)} collective-permute-done((s32[1024]{0:T(1024)S(1)}, s32[1024]{0:T(1024)S(1)}, u32[]{:S(2)}, u32[]{:S(2)}) %collective-permute-start) | collective-permute-done | bytes 4128 | tf_op jit(solution)/shard_map/while/body/eval_jaxpr/ppermute | solution.py:12
  202.6 4.1 %while.66 = (s32[]{:T(128)}, f32[2,512]{1,0:T(2,128)S(1)}, f32[2,1024]{1,0:T(2,128)S(1)}, s32[2,512]{1,0:T(2,128)S(1)}, s32[1024]{0:T(1024)S(1)}, /*index=5*/s32...) while((s32[]{:T(128)}, f32[2,512]{1,0:T(2,128)S(1)}, ...), condition=%wide.region_15.15_spmd, body=%wide.region_12.14_spmd.sunk | while | flops 810548224 | bytes 2401405 | solution.py:50
  202.6 1.9 select_reduce_fusion.7
  204.7 1.9 select_reduce_fusion.7
  206.7 1.2 copy.48
  207.9 0.1 collective-permute-start
  208.0 0.1 collective-permute-start.1
  208.2 36.1 %collective-permute-done = s32[1024]{0:T(1024)S(1)} collective-permute-done((s32[1024]{0:T(1024)S(1)}, s32[1024]{0:T(1024)S(1)}, u32[]{:S(2)}, u32[]{:S(2)}) %collective-permute-start) | collective-permute-done | bytes 4128 | tf_op jit(solution)/shard_map/while/body/eval_jaxpr/ppermute | solution.py:12
  244.3 4.1 %while.66 = (s32[]{:T(128)}, f32[2,512]{1,0:T(2,128)S(1)}, f32[2,1024]{1,0:T(2,128)S(1)}, s32[2,512]{1,0:T(2,128)S(1)}, s32[1024]{0:T(1024)S(1)}, /*index=5*/s32...) while((s32[]{:T(128)}, f32[2,512]{1,0:T(2,128)S(1)}, ...), condition=%wide.region_15.15_spmd, body=%wide.region_12.14_spmd.sunk | while | flops 810548224 | bytes 2401405 | solution.py:50
  244.3 1.9 select_reduce_fusion.7
  246.4 1.9 select_reduce_fusion.7
  248.5 1.2 copy.48
  249.6 0.1 collective-permute-start.4
  249.7 4.5 %collective-permute-done.4 = f32[1024]{0:T(1024)S(1)} collective-permute-done((f32[1024]{0:T(1024)S(1)}, f32[1024]{0:T(1024)S(1)}, u32[]{:S(2)}, u32[]{:S(2)}) %collective-permute-start.4) | collective-permute-done | bytes 4128 | tf_op jit(solution)/shard_map/ppermute | solution.py:12
  254.2 0.6 maximum_maximum_fusion
  (108 shorter events, 1.5 us)
Async XLA Ops:
  0.0 24.2 %copy-start = (bf16[512,768]{1,0:T(8,128)(2,1)S(1)}, bf16[512,768]{1,0:T(8,128)(2,1)}, u32[]{:S(2)}) copy-start(bf16[512,768]{1,0:T(8,128)(2,1)} %param.11) | copy-start | bytes 2359300
  6.4 14.5 %all-to-all-start.1 = ((s32[32,32,1]{1,2,0:T(1,128)}), s32[32,32,1]{1,2,0:T(1,128)S(1)}, u32[]{:S(2)}, u32[]{:S(2)}) async-start(s32[32,32,1]{1,2,0:T(1,128)} %all_to_all.27), calls=%async_computation.1 | async-start | bytes 32768 | tf_op jit(solution)/shard_map/all_to_all | solution.py:83
  20.9 10.5 %all-to-all-start = ((s32[32,32,1]{1,2,0:T(1,128)}), s32[32,32,1]{1,2,0:T(1,128)S(1)}, u32[]{:S(2)}, u32[]{:S(2)}) async-start(s32[32,32,1]{1,2,0:T(1,128)} %all_to_all.24), calls=%async_computation | async-start | bytes 32768 | tf_op jit(solution)/shard_map/all_to_all | solution.py:82
  31.4 41.5 %all-to-all-start.2 = ((bf16[32,32,768]{2,1,0:T(8,128)(2,1)}), bf16[32,32,768]{2,1,0:T(8,128)(2,1)S(1)}, u32[]{:S(2)}, u32[]{:S(2)}) async-start(bf16[32,32,768]{2,1,0:T(8,128)(2,1)} %bitcast.11), calls=%async_computation.2 | async-start | bytes 3145728 | tf_op jit(solution)/shard_map/all_to_all | solution.py:81
  76.7 0.6 copy-start.1
  76.7 0.6 copy-start.2
  77.3 39.1 %collective-permute-start.2 = (bf16[1024,768]{1,0:T(8,128)(2,1)}, bf16[1024,768]{1,0:T(8,128)(2,1)S(1)}, u32[]{:S(2)}, u32[]{:S(2)}) collective-permute-start(bf16[1024,768]{1,0:T(8,128)(2,1)} %get-tuple-element.668), channel_id=1, source_target_pairs={{7,0},{0,1},{1,2},{2,3},{3,4},{4,5},{5,6},{6,7},{15,8},{8,9},{9,10... | collective-permute-start | bytes 4718600 | tf_op jit(solution)/shard_map/while/body/eval_jaxpr/ppermute | solution.py:12
  77.8 38.6 %collective-permute-start = (s32[1024]{0:T(1024)S(1)}, s32[1024]{0:T(1024)S(1)}, u32[]{:S(2)}, u32[]{:S(2)}) collective-permute-start(s32[1024]{0:T(1024)S(1)} %get-tuple-element.669), channel_id=1, source_target_pairs={{7,0},{0,1},{1,2},{2,3},{3,4},{4,5},{5,6},{6,7},{15,8},{8,9},{9,10... | collective-permute-start | bytes 12296 | tf_op jit(solution)/shard_map/while/body/eval_jaxpr/ppermute | solution.py:12
  78.3 38.1 %collective-permute-start.1 = (s32[1024]{0:T(1024)S(1)}, s32[1024]{0:T(1024)S(1)}, u32[]{:S(2)}, u32[]{:S(2)}) collective-permute-start(s32[1024]{0:T(1024)S(1)} %get-tuple-element.670), channel_id=1, source_target_pairs={{7,0},{0,1},{1,2},{2,3},{3,4},{4,5},{5,6},{6,7},{15,8},{8,9},{9,10... | collective-permute-start | bytes 12296 | tf_op jit(solution)/shard_map/while/body/eval_jaxpr/ppermute | solution.py:12
  78.3 43.5 %collective-permute-start.3 = (f32[1024]{0:T(1024)S(1)}, f32[1024]{0:T(1024)S(1)}, u32[]{:S(2)}, u32[]{:S(2)}) collective-permute-start(f32[1024]{0:T(1024)S(1)} %broadcast_select_fusion.3), channel_id=1, source_target_pairs={{7,0},{0,1},{1,2},{2,3},{3,4},{4,5},{5,6},{6,7},{15,8},{8,9},{9,10... | collective-permute-start | bytes 12296 | tf_op jit(solution)/shard_map/while/body/eval_jaxpr/ppermute | solution.py:12
  121.8 38.2 %collective-permute-start.2 = (bf16[1024,768]{1,0:T(8,128)(2,1)}, bf16[1024,768]{1,0:T(8,128)(2,1)S(1)}, u32[]{:S(2)}, u32[]{:S(2)}) collective-permute-start(bf16[1024,768]{1,0:T(8,128)(2,1)} %get-tuple-element.668), channel_id=1, source_target_pairs={{7,0},{0,1},{1,2},{2,3},{3,4},{4,5},{5,6},{6,7},{15,8},{8,9},{9,10... | collective-permute-start | bytes 4718600 | tf_op jit(solution)/shard_map/while/body/eval_jaxpr/ppermute | solution.py:12
  121.8 38.1 %collective-permute-start = (s32[1024]{0:T(1024)S(1)}, s32[1024]{0:T(1024)S(1)}, u32[]{:S(2)}, u32[]{:S(2)}) collective-permute-start(s32[1024]{0:T(1024)S(1)} %get-tuple-element.669), channel_id=1, source_target_pairs={{7,0},{0,1},{1,2},{2,3},{3,4},{4,5},{5,6},{6,7},{15,8},{8,9},{9,10... | collective-permute-start | bytes 12296 | tf_op jit(solution)/shard_map/while/body/eval_jaxpr/ppermute | solution.py:12
  122.1 37.9 %collective-permute-start.1 = (s32[1024]{0:T(1024)S(1)}, s32[1024]{0:T(1024)S(1)}, u32[]{:S(2)}, u32[]{:S(2)}) collective-permute-start(s32[1024]{0:T(1024)S(1)} %get-tuple-element.670), channel_id=1, source_target_pairs={{7,0},{0,1},{1,2},{2,3},{3,4},{4,5},{5,6},{6,7},{15,8},{8,9},{9,10... | collective-permute-start | bytes 12296 | tf_op jit(solution)/shard_map/while/body/eval_jaxpr/ppermute | solution.py:12
  122.1 43.2 %collective-permute-start.3 = (f32[1024]{0:T(1024)S(1)}, f32[1024]{0:T(1024)S(1)}, u32[]{:S(2)}, u32[]{:S(2)}) collective-permute-start(f32[1024]{0:T(1024)S(1)} %broadcast_select_fusion.3), channel_id=1, source_target_pairs={{7,0},{0,1},{1,2},{2,3},{3,4},{4,5},{5,6},{6,7},{15,8},{8,9},{9,10... | collective-permute-start | bytes 12296 | tf_op jit(solution)/shard_map/while/body/eval_jaxpr/ppermute | solution.py:12
  165.3 37.3 %collective-permute-start.2 = (bf16[1024,768]{1,0:T(8,128)(2,1)}, bf16[1024,768]{1,0:T(8,128)(2,1)S(1)}, u32[]{:S(2)}, u32[]{:S(2)}) collective-permute-start(bf16[1024,768]{1,0:T(8,128)(2,1)} %get-tuple-element.668), channel_id=1, source_target_pairs={{7,0},{0,1},{1,2},{2,3},{3,4},{4,5},{5,6},{6,7},{15,8},{8,9},{9,10... | collective-permute-start | bytes 4718600 | tf_op jit(solution)/shard_map/while/body/eval_jaxpr/ppermute | solution.py:12
  165.3 37.2 %collective-permute-start = (s32[1024]{0:T(1024)S(1)}, s32[1024]{0:T(1024)S(1)}, u32[]{:S(2)}, u32[]{:S(2)}) collective-permute-start(s32[1024]{0:T(1024)S(1)} %get-tuple-element.669), channel_id=1, source_target_pairs={{7,0},{0,1},{1,2},{2,3},{3,4},{4,5},{5,6},{6,7},{15,8},{8,9},{9,10... | collective-permute-start | bytes 12296 | tf_op jit(solution)/shard_map/while/body/eval_jaxpr/ppermute | solution.py:12
  165.4 37.2 %collective-permute-start.1 = (s32[1024]{0:T(1024)S(1)}, s32[1024]{0:T(1024)S(1)}, u32[]{:S(2)}, u32[]{:S(2)}) collective-permute-start(s32[1024]{0:T(1024)S(1)} %get-tuple-element.670), channel_id=1, source_target_pairs={{7,0},{0,1},{1,2},{2,3},{3,4},{4,5},{5,6},{6,7},{15,8},{8,9},{9,10... | collective-permute-start | bytes 12296 | tf_op jit(solution)/shard_map/while/body/eval_jaxpr/ppermute | solution.py:12
  165.5 42.4 %collective-permute-start.3 = (f32[1024]{0:T(1024)S(1)}, f32[1024]{0:T(1024)S(1)}, u32[]{:S(2)}, u32[]{:S(2)}) collective-permute-start(f32[1024]{0:T(1024)S(1)} %broadcast_select_fusion.3), channel_id=1, source_target_pairs={{7,0},{0,1},{1,2},{2,3},{3,4},{4,5},{5,6},{6,7},{15,8},{8,9},{9,10... | collective-permute-start | bytes 12296 | tf_op jit(solution)/shard_map/while/body/eval_jaxpr/ppermute | solution.py:12
  207.9 36.4 %collective-permute-start.2 = (bf16[1024,768]{1,0:T(8,128)(2,1)}, bf16[1024,768]{1,0:T(8,128)(2,1)S(1)}, u32[]{:S(2)}, u32[]{:S(2)}) collective-permute-start(bf16[1024,768]{1,0:T(8,128)(2,1)} %get-tuple-element.668), channel_id=1, source_target_pairs={{7,0},{0,1},{1,2},{2,3},{3,4},{4,5},{5,6},{6,7},{15,8},{8,9},{9,10... | collective-permute-start | bytes 4718600 | tf_op jit(solution)/shard_map/while/body/eval_jaxpr/ppermute | solution.py:12
  207.9 36.3 %collective-permute-start = (s32[1024]{0:T(1024)S(1)}, s32[1024]{0:T(1024)S(1)}, u32[]{:S(2)}, u32[]{:S(2)}) collective-permute-start(s32[1024]{0:T(1024)S(1)} %get-tuple-element.669), channel_id=1, source_target_pairs={{7,0},{0,1},{1,2},{2,3},{3,4},{4,5},{5,6},{6,7},{15,8},{8,9},{9,10... | collective-permute-start | bytes 12296 | tf_op jit(solution)/shard_map/while/body/eval_jaxpr/ppermute | solution.py:12
  208.0 36.3 %collective-permute-start.1 = (s32[1024]{0:T(1024)S(1)}, s32[1024]{0:T(1024)S(1)}, u32[]{:S(2)}, u32[]{:S(2)}) collective-permute-start(s32[1024]{0:T(1024)S(1)} %get-tuple-element.670), channel_id=1, source_target_pairs={{7,0},{0,1},{1,2},{2,3},{3,4},{4,5},{5,6},{6,7},{15,8},{8,9},{9,10... | collective-permute-start | bytes 12296 | tf_op jit(solution)/shard_map/while/body/eval_jaxpr/ppermute | solution.py:12
  208.1 41.6 %collective-permute-start.3 = (f32[1024]{0:T(1024)S(1)}, f32[1024]{0:T(1024)S(1)}, u32[]{:S(2)}, u32[]{:S(2)}) collective-permute-start(f32[1024]{0:T(1024)S(1)} %broadcast_select_fusion.3), channel_id=1, source_target_pairs={{7,0},{0,1},{1,2},{2,3},{3,4},{4,5},{5,6},{6,7},{15,8},{8,9},{9,10... | collective-permute-start | bytes 12296 | tf_op jit(solution)/shard_map/while/body/eval_jaxpr/ppermute | solution.py:12
  249.6 4.6 %collective-permute-start.4 = (f32[1024]{0:T(1024)S(1)}, f32[1024]{0:T(1024)S(1)}, u32[]{:S(2)}, u32[]{:S(2)}) collective-permute-start(f32[1024]{0:T(1024)S(1)} %get-tuple-element.252), channel_id=1, source_target_pairs={{4,0},{5,1},{6,2},{7,3},{0,4},{1,5},{2,6},{3,7},{12,8},{13,9},{14,... | collective-permute-start | bytes 12296 | tf_op jit(solution)/shard_map/ppermute | solution.py:12
where the time goes:
time: 256 us; the launch traced here: 255 us
  waiting for transfers between devices  195 us (76%)
  matrix products  17.9 us (7%)
  starting transfers between devices  16 us (6%)
  local copies, waits for them, and re-layouts  15 us (6%)
  other arithmetic  10.2 us (4%)
    ppermute x17, waiting for transfers between devices, from_behind(): return lax.ppermute(block, axis, route)  153 us
    all_to_all x1, waiting for transfers between devices, local(): lax.all_to_all(send_units, ('grp', 'mem'), split_axis=0, concat_axis=0, t...  36.6 us
    dot_general x10, matrix products, block_max(): jnp.einsum('ik,jk->ij', block_units, piece_units, preferred_element_type=...  17.9 us
    all_to_all x1, starting transfers between devices, local(): lax.all_to_all(send_order, ('grp', 'mem'), split_axis=0, concat_axis=0, t...  7.33 us
  transfers between devices with their start and end apart: 20, of which 8 were waited for; matrix products, arithmetic and copies ran while one was open for 12% of the time, Pallas kernels for 0%

commit v1 on v0

v1 whole, which is shorter than its diff:
```python
import functools
import math

import jax
import jax.numpy as jnp
from jax import lax
from jax.experimental import pallas as pl
from jax.experimental.pallas import tpu as pltpu
from jax.sharding import PartitionSpec as P

MESH = pl.DeviceIdType.MESH
NZ = 4
CHUNKS = 4
TILE = 256
LOW = -2.0


def flip(index, mask):
    out, bit = index, 1
    while bit <= mask:
        if mask & bit:
            out = out + bit - 2 * bit * (lax.div(index, bit) % 2)
        bit *= 2
    return out


def kernel(
    groups, ys, units, meta, best, planes, zs, plane_meta, z_meta, col_acc, row_acc,
    row_key, row_cluster, back, z_back, z_send, ready_sem, p_send, p_recv, z_ssem, z_rsem,
    pm_send, pm_recv, zm_send, zm_recv, b_send, b_recv, zb_send, zb_recv, relay_sem,
):
    g, m = lax.axis_index("grp"), lax.axis_index("mem")
    z, y = lax.div(m, ys), m % ys
    tiles = (groups // 2) * ys
    count = 2 * tiles
    rows = planes.shape[1]
    part = rows // CHUNKS

    def plane_peer(d):
        j, c = d // 2, d % 2
        return (flip(g, (j // ys) * 2 + c), z * ys + flip(y, j % ys))

    def column_peer(dz):
        return (g, ((z + dz) % NZ) * ys + y)

    load = pltpu.make_async_copy(units, planes.at[0], ready_sem)
    load.start()

    barrier = pltpu.get_barrier_semaphore()
    peers = [plane_peer(d) for d in range(1, count)] + [column_peer(k) for k in range(1, NZ)]
    for peer in peers:
        pl.semaphore_signal(barrier, inc=1, device_id=peer, device_id_type=MESH)
    col_acc[...] = jnp.full(col_acc.shape, LOW, jnp.float32)
    row_acc[...] = jnp.full(row_acc.shape, LOW, jnp.float32)
    plane_meta[0] = meta[...]
    load.wait()
    pl.semaphore_wait(barrier, len(peers))

    def remote(src, dst, ssem, rsem, peer):
        return pltpu.make_async_remote_copy(
            src_ref=src, dst_ref=dst, send_sem=ssem, recv_sem=rsem,
            device_id=peer, device_id_type=MESH,
        )

    def piece(k):
        return pl.ds(k * part, part)

    def own_to_z(k, slot, dz):
        return remote(
            planes.at[0, piece(k)], zs.at[slot, piece(k)], z_ssem.at[slot, k],
            z_rsem.at[slot, k], column_peer(dz),
        )

    def relay(k, src, dst, dz):
        return remote(
            zs.at[src, piece(k)], zs.at[dst, piece(k)], relay_sem.at[src, k],
            z_rsem.at[dst, k], column_peer(dz),
        )

    def to_plane(d):
        return remote(planes.at[0], planes.at[d], p_send.at[d], p_recv.at[d], plane_peer(d))

    def forward(j):
        return remote(
            planes.at[2 * j], planes.at[2 * j + 1], p_send.at[2 * j + 1], p_recv.at[2 * j + 1],
            plane_peer(1),
        )

    meta_copies = [
        remote(meta, plane_meta.at[d], pm_send.at[d], pm_recv.at[d], plane_peer(d))
        for d in range(1, count)
    ] + [
        remote(meta, z_meta.at[s], zm_send.at[s], zm_recv.at[s], column_peer(-1 - s))
        for s in range(2)
    ]
    for copy in meta_copies:
        copy.start()

    to_plane(1).start()

    @pl.when(z >= 1)
    def _():
        for k in range(CHUNKS):
            own_to_z(k, 0, -1).start()

    @pl.when(z <= 1)
    def _():
        for k in range(CHUNKS):
            own_to_z(k, 1, 2).start()

    for j in range(1, tiles):
        to_plane(2 * j).start()

    def spread(a, source):
        row_key[a] = jnp.broadcast_to(source[0:1, :], (128, rows)).T
        row_cluster[a] = jnp.broadcast_to(source[1:2, :], (128, rows)).T

    def pairs(a, left, d, both):
        right = planes[d]
        keys, clusters = plane_meta[d, 0:1, :], plane_meta[d, 1:2, :]

        def step(i, carry):
            here = pl.ds(pl.multiple_of(i * TILE, TILE), TILE)
            scores = lax.dot_general(
                left[here, :], right, (((1,), (1,)), ((), ())),
                preferred_element_type=jnp.float32,
            )
            my_key, my_cluster = row_key[a, here, :], row_cluster[a, here, :]
            acc = row_acc[a, here, :]
            for t in range(rows // 128):
                lanes = slice(t * 128, (t + 1) * 128)
                kept = jnp.where(my_cluster == clusters[:, lanes], scores[:, lanes], LOW)
                earlier = keys[:, lanes] < my_key
                acc = jnp.maximum(acc, jnp.where(earlier, kept, LOW))
                if both:
                    other = jnp.where(earlier, LOW, kept).reshape(TILE // 8, 8, 128)
                    col_acc[d, :, lanes] = jnp.maximum(col_acc[d, :, lanes], jnp.max(other, axis=0))
            row_acc[a, here, :] = acc
            return carry

        lax.fori_loop(0, rows // TILE, step, 0)

    spread(0, meta)
    own = planes.at[0]
    pairs(0, own, 0, False)
    for copy in meta_copies:
        copy.wait()
    to_plane(1).wait_recv()
    pairs(0, own, 1, False)

    for k in range(CHUNKS):
        @pl.when((z == 1) | (z == 2))
        def _():
            own_to_z(k, 0, -1).wait_recv()
            relay(k, 0, 1, -1).start()

        @pl.when(z == 2)
        def _():
            own_to_z(k, 1, 2).wait_recv()
            relay(k, 1, 0, 1).start()

    def plane_step(j, carry):
        pltpu.make_async_copy(planes.at[2 * j], planes.at[2 * j], p_recv.at[2 * j]).wait()
        forward(j).start()
        pairs(0, own, 2 * j, False)
        forward(j).wait_recv()
        pairs(0, own, 2 * j + 1, False)
        return carry

    lax.fori_loop(1, tiles, plane_step, 0)

    for k in range(CHUNKS):
        @pl.when((z == 0) | (z == 3))
        def _():
            own_to_z(k, 0, -1).wait_recv()

        @pl.when(z != 2)
        def _():
            own_to_z(k, 1, 2).wait_recv()

    spread(1, z_meta.at[0])
    spread(2, z_meta.at[1])

    def z1_step(d, carry):
        pairs(1, zs.at[0], d, True)
        return carry

    lax.fori_loop(0, count, z1_step, 0)
    first = lax.div(z, 2) * (count // 2)

    def z2_step(d, carry):
        pairs(2, zs.at[1], d + first, True)
        return carry

    lax.fori_loop(0, count // 2, z2_step, 0)

    def fold(a):
        return jnp.max(row_acc[a].T.reshape(16, 8, rows), axis=0)

    z_send[0] = fold(1)
    z_send[1] = fold(2)
    result_copies = [
        remote(col_acc.at[d], back.at[d], b_send.at[d], b_recv.at[d], plane_peer(d))
        for d in range(1, count)
    ]
    for copy in result_copies:
        copy.start()
    mine = jnp.maximum(fold(0), col_acc[0])
    z_copies = [
        remote(z_send.at[s], z_back.at[s], zb_send.at[s], zb_recv.at[s], column_peer(1 + s))
        for s in range(2)
    ]
    for copy in z_copies:
        copy.start()

    @pl.when(z >= 1)
    def _():
        for k in range(CHUNKS):
            own_to_z(k, 0, -1).wait_send()

    @pl.when(z <= 1)
    def _():
        for k in range(CHUNKS):
            own_to_z(k, 1, 2).wait_send()

    @pl.when((z == 1) | (z == 2))
    def _():
        for k in range(CHUNKS):
            relay(k, 0, 1, -1).wait_send()

    @pl.when(z == 2)
    def _():
        for k in range(CHUNKS):
            relay(k, 1, 0, 1).wait_send()

    to_plane(1).wait_send()
    for j in range(1, tiles):
        to_plane(2 * j).wait_send()
        forward(j).wait_send()

    for copy in result_copies + z_copies:
        copy.wait()
    for d in range(1, count):
        mine = jnp.maximum(mine, back[d])
    mine = jnp.maximum(mine, jnp.maximum(z_back[0], z_back[1]))
    best[...] = jnp.maximum(jnp.max(mine, axis=0, keepdims=True), -1.0)


def similarities(units, meta, groups, members):
    rows, width = units.shape
    ys = members // NZ
    count = groups * ys
    dma = pltpu.SemaphoreType.DMA
    return pl.pallas_call(
        functools.partial(kernel, groups, ys),
        out_shape=jax.ShapeDtypeStruct((1, rows), jnp.float32),
        in_specs=[
            pl.BlockSpec(memory_space=pl.ANY),
            pl.BlockSpec(memory_space=pltpu.VMEM),
        ],
        out_specs=pl.BlockSpec(memory_space=pltpu.VMEM),
        scratch_shapes=[
            pltpu.VMEM((count, rows, width), jnp.bfloat16),
            pltpu.VMEM((2, rows, width), jnp.bfloat16),
            pltpu.VMEM((count, 2, rows), jnp.float32),
            pltpu.VMEM((2, 2, rows), jnp.float32),
            pltpu.VMEM((count, 8, rows), jnp.float32),
            pltpu.VMEM((3, rows, 128), jnp.float32),
            pltpu.VMEM((3, rows, 128), jnp.float32),
            pltpu.VMEM((3, rows, 128), jnp.float32),
            pltpu.VMEM((count, 8, rows), jnp.float32),
            pltpu.VMEM((2, 8, rows), jnp.float32),
            pltpu.VMEM((2, 8, rows), jnp.float32),
            dma(()),
            dma((count,)), dma((count,)),
            dma((2, CHUNKS)), dma((2, CHUNKS)),
            dma((count,)), dma((count,)),
            dma((2,)), dma((2,)),
            dma((count,)), dma((count,)),
            dma((2,)), dma((2,)),
            dma((2, CHUNKS)),
        ],
        compiler_params=pltpu.CompilerParams(
            collective_id=0, has_side_effects=True, vmem_limit_bytes=56 * 1024 * 1024
        ),
    )(units, meta)


def local(embeddings, cluster_id, row_order, assignment, placement):
    members = lax.axis_size("mem")
    groups = lax.axis_size("grp")
    owners = groups * members
    row_count, feature_count = embeddings.shape
    capacity = max(2, 2 * row_count // owners)
    widened = embeddings.astype(jnp.float32)
    unit_rows = (
        widened
        * lax.rsqrt(jnp.mean(widened * widened, axis=1, keepdims=True) + 1e-06)
        * (1.0 / math.sqrt(feature_count))
    ).astype(jnp.bfloat16)
    meta = jnp.stack([row_order, cluster_id]).astype(jnp.float32)
    best = similarities(unit_rows, meta, groups, members)

    table_hits = cluster_id[:, None] == jnp.arange(assignment.shape[0], dtype=jnp.int32)[None, :]
    group_of = jnp.sum(jnp.where(table_hits, assignment[None, :], 0), axis=1)
    owner_id = group_of * members + placement
    before = jnp.arange(row_count)[None, :] < jnp.arange(row_count)[:, None]
    rank = jnp.sum((before & (owner_id[None, :] == owner_id[:, None])).astype(jnp.int32), axis=1)
    target = owner_id * capacity + rank
    slots = jnp.arange(owners * capacity, dtype=jnp.int32)
    filled = jnp.max(
        jnp.where(slots[:, None] == target[None, :], best, -1.0), axis=1
    )
    return lax.all_to_all(filled, ("grp", "mem"), split_axis=0, concat_axis=0, tiled=True)


def solution(mesh):
    return jax.shard_map(
        local,
        mesh=mesh,
        in_specs=(
            P(("grp", "mem"), None),
            P(("grp", "mem")),
            P(("grp", "mem")),
            P(),
            P(("grp", "mem")),
        ),
        out_specs=P(("grp", "mem")),
        check_vma=False,
    )
```

time: 256 us -> 80.5 us (0.31)
  waiting for transfers between devices: 195 us -> 0 us
  Pallas kernels: 0 us -> 63.8 us
  matrix products: 17.9 us -> 0 us
  starting transfers between devices: 16 us -> 0 us
  local copies, waits for them, and re-layouts: 15 us -> 1.27 us
  blocking collectives: 0 us -> 9.99 us
  other arithmetic: 10.2 us -> 5.17 us
    ppermute x17 -> x0, waiting for transfers between devices: 153 us -> none  [from_behind(): return lax.ppermute(block, axis, route)]
    pallas_call x0 -> x1, Pallas kernels: none -> 63.8 us  [similarities(): pl.pallas_call(functools.partial(kernel, groups, ys), out_shape=jax.Shape...]
    all_to_all x3 -> x0, waiting for transfers between devices: 42.3 us -> none  [the longest x1 36.6 us: local(): lax.all_to_all(send_units, ('grp', 'mem'), split_axis=0, concat_axis=0, t...]
    dot_general x10 -> x0, matrix products: 17.9 us -> none  [block_max(): jnp.einsum('ik,jk->ij', block_units, piece_units, preferred_element_type=...]
    all_to_all x3 -> x0, starting transfers between devices: 13.4 us -> none  [the longest x1 7.33 us: local(): lax.all_to_all(send_order, ('grp', 'mem'), split_axis=0, concat_axis=0, t...]
    all_to_all x0 -> x1, blocking collectives: none -> 9.99 us  [local(): lax.all_to_all(filled, ('grp', 'mem'), split_axis=0, concat_axis=0, tiled...]
    scatter x2 -> x0, local copies, waits for them, and re-layouts: 5.21 us -> none  [the longest x1 2.6 us: local(): send_order = jnp.zeros((slot_count,), jnp.int32).at[target].set(row_order)]
    while x16 -> x0, local copies, waits for them, and re-layouts: 4.64 us -> none
  transfers between devices with their start and end apart: 20 -> 0, of which waited for: 8 -> 0; matrix products, arithmetic and copies ran while one was open for 12% -> 0% of each run, Pallas kernels for 0% -> 0%
where the time goes in v1:
time: 80.5 us; the launch traced here: 80.3 us
  Pallas kernels  63.8 us (79%)
  blocking collectives  9.99 us (12%)
  other arithmetic  5.17 us (6%)
  local copies, waits for them, and re-layouts  1.27 us (2%)
    pallas_call x1, Pallas kernels, similarities(): pl.pallas_call(functools.partial(kernel, groups, ys), out_shape=jax.Shape...  63.8 us
    all_to_all x1, blocking collectives, local(): lax.all_to_all(filled, ('grp', 'mem'), split_axis=0, concat_axis=0, tiled...  9.99 us

profile of v1, /device:TPU:0, one launch (start us, length us, event | category | flops | bytes accessed | tf_op | source)
XLA Modules:
  0.0 80.3 jit_solution(793526906186711191)
XLA Ops:
  0.0 0.0 copy-start
  0.0 1.4 %fusion = f32[512]{0:T(512)S(1)} fusion(bf16[512,768]{1,0:T(8,128)(2,1)} %param.5), kind=kLoop, calls=%fused_computation.4 | loop fusion | flops 1179136 | bytes 788480 | tf_op jit(solution)/shard_map/reduce_sum | solution.py:298
  1.4 0.0 copy-done
  1.5 0.0 copy-start.1
  1.5 0.0 copy-start.4
  1.5 0.0 copy-start.2
  1.5 0.0 copy-start.3
  1.5 1.1 %fusion.2.units = bf16[512,768]{1,0:T(8,128)(2,1)} fusion(bf16[512,768]{1,0:T(8,128)(2,1)S(1)} %copy-done, f32[512]{0:T(512)S(1)} %add_rsqrt_fusion), kind=kLoop, calls=%fused_computation.6 | loop fusion | flops 1572864 | bytes 1574912 | tf_op jit(solution)/shard_map/convert_element_type | solution.py:300
  2.6 0.0 copy-done.1
  2.6 0.0 copy-done.4
  2.6 0.1 select_reduce_fusion.1
  2.7 0.0 copy-done.2
  2.7 0.3 convert_reduce_fusion
  3.0 0.0 copy-done.3
  3.0 0.6 add_convert_fusion.meta
  3.6 63.8 %shard_map.55 = f32[1,512]{1,0:T(1,128)} custom-call(bf16[512,768]{1,0:T(8,128)(2,1)} %fusion.2.units, f32[2,512]{1,0:T(2,128)} %add_convert_fusion.meta), custom_call_target="tpu_custom_call" | custom-call | tf_op jit(solution)/shard_map/pallas_call | solution.py:254
  67.4 1.0 %select_reduce_fusion = f32[1024]{0:T(1024)S(1)} fusion(f32[512]{0:T(512)} %bitcast.6, s32[512]{0:T(512)S(1)} %multiply_add_fusion), kind=kLoop, calls=%fused_computation | loop fusion | flops 1571840 | bytes 8192 | tf_op jit(solution)/shard_map/reduce_max | solution.py:311
  68.3 0.1 all_to_all.8
  68.4 10.0 %all_to_all.12 = f32[32,32,1]{1,2,0:T(1,128)S(1)} all-to-all(f32[32,32,1]{1,2,0:T(1,128)S(1)} %bitcast.5), channel_id=1, replica_groups=mesh['grp'=4,'mem'=8] {'grp','mem'}, dimensions={0} | all-to-all | bytes 8192 | tf_op jit(solution)/shard_map/all_to_all | solution.py:314
  78.4 0.5 broadcast.19
  78.9 0.7 reduce.3
  79.6 0.7 all_to_all.10
  (3 shorter events, 0.0 us)
Async XLA Ops:
  0.0 1.4 %copy-start = (bf16[512,768]{1,0:T(8,128)(2,1)S(1)}, bf16[512,768]{1,0:T(8,128)(2,1)}, u32[]{:S(2)}) copy-start(bf16[512,768]{1,0:T(8,128)(2,1)} %param.5) | copy-start | bytes 2359300
  1.5 1.2 %copy-start.1 = (s32[512]{0:T(512)S(1)}, s32[512]{0:T(512)}, u32[]{:S(2)}) copy-start(s32[512]{0:T(512)} %param.6) | copy-start | bytes 6148
  1.5 1.2 %copy-start.4 = (s32[4]{0:T(128)S(1)}, s32[4]{0:T(128)}, u32[]{:S(2)}) copy-start(s32[4]{0:T(128)} %param.8) | copy-start | bytes 52
  1.5 1.2 %copy-start.2 = (s32[512]{0:T(512)S(1)}, s32[512]{0:T(512)}, u32[]{:S(2)}) copy-start(s32[512]{0:T(512)} %param.9) | copy-start | bytes 6148
  1.5 1.5 %copy-start.3 = (s32[512]{0:T(512)S(1)}, s32[512]{0:T(512)}, u32[]{:S(2)}) copy-start(s32[512]{0:T(512)} %param.7) | copy-start | bytes 6148

commit v2 on v1

v2 whole, which is shorter than its diff:
```python
import functools
import math

import jax
import jax.numpy as jnp
from jax import lax
from jax.experimental import pallas as pl
from jax.experimental.pallas import tpu as pltpu
from jax.sharding import PartitionSpec as P

MESH = pl.DeviceIdType.MESH
NZ = 4
CHUNKS = 8
LOW = -2.0


def flip(index, mask):
    out, bit = index, 1
    while bit <= mask:
        if mask & bit:
            out = out + bit - 2 * bit * (lax.div(index, bit) % 2)
        bit *= 2
    return out


def kernel(
    groups, members, rows_in, meta, target, out, planes, zs, plane_meta, z_meta, col_acc,
    row_acc, row_key, row_cluster, back, z_back, z_send, slot_send, slot_recv, p_send, p_recv,
    h_send, h_recv, z_ssem, z_rsem, pm_send, pm_recv, zm_send, zm_recv, b_send, b_recv,
    zb_send, zb_recv, relay_sem, s_send, s_recv,
):
    ys = members // NZ
    g, m = lax.axis_index("grp"), lax.axis_index("mem")
    z, y = lax.div(m, ys), m % ys
    me = g * members + m
    owners = groups * members
    tiles = (groups // 2) * ys
    count = 2 * tiles
    half = count // 2
    rows, width = planes.shape[1], planes.shape[2]
    part = rows // CHUNKS
    square = tiles == 4 and ys == 2
    capacity = out.shape[1]
    shared = 128 // capacity

    def plane_peer(d):
        j, c = d // 2, d % 2
        return (flip(g, (j // ys) * 2 + c), z * ys + flip(y, j % ys))

    def column_peer(dz):
        return (g, ((z + dz) % NZ) * ys + y)

    def other_device(r):
        o = (me + r) % owners
        return o, (lax.div(o, members), o % members)

    barrier = pltpu.get_barrier_semaphore()

    def greet(r, carry):
        pl.semaphore_signal(
            barrier, inc=1, device_id=other_device(r)[1], device_id_type=MESH
        )
        return carry

    lax.fori_loop(1, owners, greet, 0)

    def normalise(i, carry):
        here = pl.ds(pl.multiple_of(i * 64, 64), 64)
        wide = rows_in[here, :].astype(jnp.float32)
        mean = jnp.sum(wide * wide, axis=1, keepdims=True) * (1.0 / width)
        scaled = wide * lax.rsqrt(mean + 1e-06) * (1.0 / math.sqrt(width))
        planes[0, here, :] = scaled.astype(jnp.bfloat16)
        return carry

    lax.fori_loop(0, rows // 64, normalise, 0)
    col_acc[...] = jnp.full(col_acc.shape, LOW, jnp.float32)
    row_acc[...] = jnp.full(row_acc.shape, LOW, jnp.float32)
    plane_meta[0] = meta[...]

    def spread(a, source):
        row_key[a] = jnp.broadcast_to(source[0:1, :], (128, rows)).T
        row_cluster[a] = jnp.broadcast_to(source[1:2, :], (128, rows)).T

    spread(0, meta)
    pl.semaphore_wait(barrier, owners - 1)

    def remote(src, dst, ssem, rsem, peer):
        return pltpu.make_async_remote_copy(
            src_ref=src, dst_ref=dst, send_sem=ssem, recv_sem=rsem,
            device_id=peer, device_id_type=MESH,
        )

    def piece(k):
        return pl.ds(k * part, part)

    def own_to_z(k, slot, dz):
        return remote(
            planes.at[0, piece(k)], zs.at[slot, piece(k)], z_ssem.at[slot, k],
            z_rsem.at[slot, k], column_peer(dz),
        )

    def relay(k, src, dst, dz):
        return remote(
            zs.at[src, piece(k)], zs.at[dst, piece(k)], relay_sem.at[src, k],
            z_rsem.at[dst, k], column_peer(dz),
        )

    def to_plane(d):
        return remote(planes.at[0], planes.at[d], p_send.at[d], p_recv.at[d], plane_peer(d))

    def diagonal(h):
        src, peer = ((2, 4), (4, 2))[h]
        rows_h = pl.ds(h * (rows // 2), rows // 2)
        return remote(
            planes.at[src, rows_h], planes.at[6, rows_h], h_send.at[h], h_recv.at[h],
            plane_peer(peer),
        )

    def forward(j):
        return remote(
            planes.at[2 * j], planes.at[2 * j + 1], p_send.at[2 * j + 1], p_recv.at[2 * j + 1],
            plane_peer(1),
        )

    meta_copies = [
        remote(meta, plane_meta.at[d], pm_send.at[d], pm_recv.at[d], plane_peer(d))
        for d in range(1, count)
    ] + [
        remote(meta, z_meta.at[s], zm_send.at[s], zm_recv.at[s], column_peer(-1 - s))
        for s in range(2)
    ]
    for copy in meta_copies:
        copy.start()

    @pl.when(z >= 1)
    def _():
        for k in range(CHUNKS):
            own_to_z(k, 0, -1).start()

    @pl.when(z <= 1)
    def _():
        for k in range(CHUNKS):
            own_to_z(k, 1, 2).start()

    direct = range(1, tiles - 1 if square else tiles)
    for j in direct:
        to_plane(2 * j).start()
    to_plane(1).start()

    def pairs(a, left, d, start, size, both):
        right = planes[d]
        keys, clusters = plane_meta[d, 0:1, :], plane_meta[d, 1:2, :]
        here = pl.ds(start, size)
        scores = lax.dot_general(
            left[here, :], right, (((1,), (1,)), ((), ())),
            preferred_element_type=jnp.float32,
        )
        my_key, my_cluster = row_key[a, here, :], row_cluster[a, here, :]
        acc = row_acc[a, here, :]
        for t in range(rows // 128):
            lanes = slice(t * 128, (t + 1) * 128)
            kept = jnp.where(my_cluster == clusters[:, lanes], scores[:, lanes], LOW)
            earlier = keys[:, lanes] < my_key
            acc = jnp.maximum(acc, jnp.where(earlier, kept, LOW))
            if both:
                other = jnp.where(earlier, LOW, kept).reshape(size // 8, 8, 128)
                col_acc[d, :, lanes] = jnp.maximum(col_acc[d, :, lanes], jnp.max(other, axis=0))
        row_acc[a, here, :] = acc

    own = planes.at[0]

    def own_pairs(d0, d1):
        def step(d, carry):
            pairs(0, own, d, 0, rows // 2, False)
            pairs(0, own, d, rows // 2, rows // 2, False)
            return carry

        lax.fori_loop(d0, d1, step, 0)

    first = lax.div(z, 2) * half

    def z_pairs(d0, d1, start, size):
        def step(d, carry):
            pairs(1, zs.at[0], d, start, size, True)

            @pl.when((d >= first) & (d < first + half))
            def _():
                pairs(2, zs.at[1], d, start, size, True)

            return carry

        lax.fori_loop(d0, d1, step, 0)

    def own_recv(k, slot):
        own_to_z(k, slot, -1).wait_recv()

    def relays_one(ks):
        @pl.when((z == 1) | (z == 2))
        def _():
            for k in ks:
                own_recv(k, 0)
                relay(k, 0, 1, -1).start()

    def arrive(ks):
        for k in ks:
            @pl.when((z == 0) | (z == 3))
            def _():
                own_recv(k, 0)

            own_recv(k, 1)

            @pl.when(z == 2)
            def _():
                relay(k, 1, 0, 1).start()

    quarter = rows // 4
    per = CHUNKS // 4

    def chunk_range(s):
        return range(s * per, (s + 1) * per)

    own_pairs(0, 1)
    for copy in meta_copies:
        copy.wait()
    to_plane(1).wait_recv()
    own_pairs(1, 2)
    spread(1, z_meta.at[0])
    spread(2, z_meta.at[1])

    relays_one(range(0, 2 * per))
    arrive(chunk_range(0))
    z_pairs(0, 2, 0, quarter)
    relays_one(range(2 * per, 4 * per))
    arrive(chunk_range(1))

    def collect(j, carry):
        pltpu.make_async_copy(planes.at[2 * j], planes.at[2 * j], p_recv.at[2 * j]).wait()
        forward(j).start()
        return carry

    def collect_partner(j, carry):
        forward(j).wait_recv()
        return carry

    lax.fori_loop(1, tiles - 1, collect, 0)
    if square:
        diagonal(0).start()
        diagonal(1).start()
    z_pairs(0, 2, quarter, quarter)
    lax.fori_loop(1, tiles - 1, collect_partner, 0)
    own_pairs(2, count - 2)
    z_pairs(2, count - 2, 0, 2 * quarter)
    arrive(chunk_range(2))
    if square:
        diagonal(0).wait_recv()
        diagonal(1).wait_recv()
        forward(tiles - 1).start()
    else:
        collect(tiles - 1, 0)
    z_pairs(0, count - 2, 2 * quarter, quarter)
    forward(tiles - 1).wait_recv()
    own_pairs(count - 2, count)
    z_pairs(count - 2, count, 0, 2 * quarter)
    z_pairs(count - 2, count, 2 * quarter, quarter)
    arrive(chunk_range(3))
    z_pairs(0, count, 3 * quarter, quarter)

    def fold(a):
        return jnp.max(row_acc[a].T.reshape(16, 8, rows), axis=0)

    z_send[0] = fold(1)
    z_send[1] = fold(2)
    result_copies = [
        remote(col_acc.at[d], back.at[d], b_send.at[d], b_recv.at[d], plane_peer(d))
        for d in range(1, count)
    ]
    for copy in result_copies:
        copy.start()
    mine = jnp.maximum(fold(0), col_acc[0])
    z_copies = [
        remote(z_send.at[s], z_back.at[s], zb_send.at[s], zb_recv.at[s], column_peer(1 + s))
        for s in range(2)
    ]
    for copy in z_copies:
        copy.start()
    wanted = jnp.broadcast_to(target[...], (128, rows)).T

    @pl.when(z >= 1)
    def _():
        for k in range(CHUNKS):
            own_to_z(k, 0, -1).wait_send()

    @pl.when(z <= 1)
    def _():
        for k in range(CHUNKS):
            own_to_z(k, 1, 2).wait_send()

    @pl.when((z == 1) | (z == 2))
    def _():
        for k in range(CHUNKS):
            relay(k, 0, 1, -1).wait_send()

    @pl.when(z == 2)
    def _():
        for k in range(CHUNKS):
            relay(k, 1, 0, 1).wait_send()

    to_plane(1).wait_send()
    for j in direct:
        to_plane(2 * j).wait_send()
    if square:
        diagonal(0).wait_send()
        diagonal(1).wait_send()
    for j in range(1, tiles):
        forward(j).wait_send()

    for copy in result_copies + z_copies:
        copy.wait()
    for d in range(1, count):
        mine = jnp.maximum(mine, back[d])
    mine = jnp.maximum(mine, jnp.maximum(z_back[0], z_back[1]))
    best = jnp.maximum(jnp.max(mine, axis=0, keepdims=True), -1.0)
    similar = jnp.broadcast_to(best, (128, rows)).T
    lane = lax.broadcasted_iota(jnp.int32, (rows, 128), 1).astype(jnp.float32)
    for t in range(slot_send.shape[0]):
        hit = jnp.where(wanted == lane + float(t * 128), similar, -1.0)
        slot_send[t] = jnp.max(hit, axis=0, keepdims=True)

    def slot_copy(r):
        o, peer = other_device(r)
        return remote(
            slot_send.at[lax.div(o, shared)], slot_recv.at[me], s_send.at[r], s_recv.at[me], peer
        )

    def send_slots(r, carry):
        slot_copy(r).start()
        return carry

    def wait_slots(r, carry):
        slot_copy(r).wait_send()
        source = (me + r) % owners
        pltpu.make_async_copy(
            slot_recv.at[source], slot_recv.at[source], s_recv.at[source]
        ).wait()
        return carry

    lax.fori_loop(1, owners, send_slots, 0)
    slot_recv[me] = slot_send[lax.div(me, shared)]
    lax.fori_loop(1, owners, wait_slots, 0)
    got = slot_recv[...].reshape(owners, 128)
    mine_at = me % shared
    picked = got[:, :capacity]
    for q in range(1, shared):
        picked = jnp.where(mine_at == q, got[:, q * capacity : (q + 1) * capacity], picked)
    out[...] = picked


def similarities(embeddings, meta, target, groups, members, capacity):
    rows, width = embeddings.shape
    ys = members // NZ
    count = groups * ys
    owners = groups * members
    dma = pltpu.SemaphoreType.DMA
    vmem = pl.BlockSpec(memory_space=pltpu.VMEM)
    return pl.pallas_call(
        functools.partial(kernel, groups, members),
        out_shape=jax.ShapeDtypeStruct((owners, capacity), jnp.float32),
        in_specs=[vmem, vmem, vmem],
        out_specs=vmem,
        scratch_shapes=[
            pltpu.VMEM((count, rows, width), jnp.bfloat16),
            pltpu.VMEM((2, rows, width), jnp.bfloat16),
            pltpu.VMEM((count, 2, rows), jnp.float32),
            pltpu.VMEM((2, 2, rows), jnp.float32),
            pltpu.VMEM((count, 8, rows), jnp.float32),
            pltpu.VMEM((3, rows, 128), jnp.float32),
            pltpu.VMEM((3, rows, 128), jnp.float32),
            pltpu.VMEM((3, rows, 128), jnp.float32),
            pltpu.VMEM((count, 8, rows), jnp.float32),
            pltpu.VMEM((2, 8, rows), jnp.float32),
            pltpu.VMEM((2, 8, rows), jnp.float32),
            pltpu.VMEM((owners * capacity // 128, 1, 128), jnp.float32),
            pltpu.VMEM((owners, 1, 128), jnp.float32),
            dma((count,)), dma((count,)),
            dma((2,)), dma((2,)),
            dma((2, CHUNKS)), dma((2, CHUNKS)),
            dma((count,)), dma((count,)),
            dma((2,)), dma((2,)),
            dma((count,)), dma((count,)),
            dma((2,)), dma((2,)),
            dma((2, CHUNKS)),
            dma((owners,)), dma((owners,)),
        ],
        compiler_params=pltpu.CompilerParams(
            collective_id=0, has_side_effects=True, vmem_limit_bytes=56 * 1024 * 1024
        ),
    )(embeddings, meta, target)


def local(embeddings, cluster_id, row_order, assignment, placement):
    members = lax.axis_size("mem")
    groups = lax.axis_size("grp")
    owners = groups * members
    row_count = embeddings.shape[0]
    capacity = max(2, 2 * row_count // owners)
    table_hits = cluster_id[:, None] == jnp.arange(assignment.shape[0], dtype=jnp.int32)[None, :]
    group_of = jnp.sum(jnp.where(table_hits, assignment[None, :], 0), axis=1)
    owner_id = group_of * members + placement
    before = jnp.arange(row_count)[None, :] < jnp.arange(row_count)[:, None]
    rank = jnp.sum((before & (owner_id[None, :] == owner_id[:, None])).astype(jnp.int32), axis=1)
    target = (owner_id * capacity + rank).astype(jnp.float32)[None, :]
    meta = jnp.stack([row_order, cluster_id]).astype(jnp.float32)
    filled = similarities(embeddings, meta, target, groups, members, capacity)
    return filled.reshape(owners * capacity)


def solution(mesh):
    return jax.shard_map(
        local,
        mesh=mesh,
        in_specs=(
            P(("grp", "mem"), None),
            P(("grp", "mem")),
            P(("grp", "mem")),
            P(),
            P(("grp", "mem")),
        ),
        out_specs=P(("grp", "mem")),
        check_vma=False,
    )
```

time: 80.5 us -> 86.9 us (1.080)
  Pallas kernels: 63.8 us -> 82.3 us
  blocking collectives: 9.99 us -> 0 us
  other arithmetic: 5.17 us -> 1.53 us
  local copies, waits for them, and re-layouts: 1.27 us -> 2.75 us
    pallas_call x1, Pallas kernels: 63.8 us -> 82.3 us  [similarities(): pl.pallas_call(functools.partial(kernel, groups, members), out_shape=jax....]
    all_to_all x1 -> x0, blocking collectives: 9.99 us -> none  [local(): lax.all_to_all(filled, ('grp', 'mem'), split_axis=0, concat_axis=0, tiled...]
    reduce_sum x1 -> x0, other arithmetic: 1.43 us -> none  [local(): jnp.mean(widened * widened, axis=1, keepdims=True) + 1e-06]
    reshape x0 -> x1, local copies, waits for them, and re-layouts: none -> 1.38 us  [local(): return filled.reshape(owners * capacity)]
    unnamed x10 -> x8, local copies, waits for them, and re-layouts: 0.03 us -> 1.37 us
    all_to_all x3 -> x0, local copies, waits for them, and re-layouts: 1.25 us -> none  [local(): lax.all_to_all(filled, ('grp', 'mem'), split_axis=0, concat_axis=0, tiled...]
    reduce_max x1 -> x0, other arithmetic: 0.97 us -> none  [local(): jnp.max(jnp.where(slots[:, None] == target[None, :], best, -1.0), axis=1)]
where the time goes in v2:
time: 86.9 us; the launch traced here: 86.6 us
  Pallas kernels  82.3 us (95%)
  local copies, waits for them, and re-layouts  2.75 us (3%)
  other arithmetic  1.53 us (2%)
    pallas_call x1, Pallas kernels, similarities(): pl.pallas_call(functools.partial(kernel, groups, members), out_shape=jax....  82.3 us

profile of v2, /device:TPU:0, one launch (start us, length us, event | category | flops | bytes accessed | tf_op | source)
XLA Modules:
  0.0 86.6 jit_solution(5411129976037938085)
XLA Ops:
  0.0 0.0 copy-start
  0.0 0.0 copy-start.3
  0.0 0.7 copy-done
  0.7 0.0 copy-done.3
  0.7 0.0 copy-start.1
  0.7 0.1 select_reduce_fusion
  0.8 0.6 copy-done.1
  1.4 0.3 convert_reduce_fusion
  1.6 0.0 copy-start.2
  1.6 0.6 add_convert_fusion.1
  2.2 0.1 copy-done.2
  2.3 0.6 add_convert_fusion.meta
  2.9 82.3 %shard_map.55 = f32[32,32]{1,0:T(8,128)} custom-call(bf16[512,768]{1,0:T(8,128)(2,1)} %rows_in.1, f32[2,512]{1,0:T(2,128)} %add_convert_fusion.meta, f32[1,512]{1,0:T(1,128)} %bitcast.3), custom_call_target="tpu_custom_call" | custom-call | tf_op jit(solution)/shard_map/pallas_call | solution.py:365
  85.3 1.4 %reshape.7 = f32[1024]{0:T(1024)} reshape(f32[32,32]{1,0:T(8,128)} %shard_map.55) | data formatting | bytes 8192 | tf_op jit(solution)/shard_map/reshape | solution.py:414
  (1 shorter events, 0.0 us)
Async XLA Ops:
  0.0 0.7 copy-start
  0.0 0.7 copy-start.3
  0.7 0.7 copy-start.1
  1.6 0.7 copy-start.2

commit v3 on v1

--- a/solution.py
+++ b/solution.py
@@ -25,16 +25,22 @@
 
 
 def kernel(
-    groups, ys, units, meta, best, planes, zs, plane_meta, z_meta, col_acc, row_acc,
-    row_key, row_cluster, back, z_back, z_send, ready_sem, p_send, p_recv, z_ssem, z_rsem,
+    groups, members, units, meta, target, out, planes, zs, plane_meta, z_meta, col_acc, row_acc,
+    row_key, row_cluster, back, z_back, z_send, slot_send, slot_recv, ready_sem, p_send, p_recv, z_ssem, z_rsem,
     pm_send, pm_recv, zm_send, zm_recv, b_send, b_recv, zb_send, zb_recv, relay_sem,
+    s_send, s_recv,
 ):
+    ys = members // NZ
     g, m = lax.axis_index("grp"), lax.axis_index("mem")
     z, y = lax.div(m, ys), m % ys
     tiles = (groups // 2) * ys
     count = 2 * tiles
     rows = planes.shape[1]
     part = rows // CHUNKS
+    me = g * members + m
+    owners = groups * members
+    capacity = out.shape[1]
+    shared = 128 // capacity
 
     def plane_peer(d):
         j, c = d // 2, d % 2
@@ -46,15 +52,25 @@
     load = pltpu.make_async_copy(units, planes.at[0], ready_sem)
     load.start()
 
+    def other_device(r):
+        o = (me + r) % owners
+        return o, (lax.div(o, members), o % members)
+
     barrier = pltpu.get_barrier_semaphore()
-    peers = [plane_peer(d) for d in range(1, count)] + [column_peer(k) for k in range(1, NZ)]
-    for peer in peers:
-        pl.semaphore_signal(barrier, inc=1, device_id=peer, device_id_type=MESH)
+
+    def greet(r, carry):
+        pl.semaphore_signal(
+            barrier, inc=1, device_id=other_device(r)[1], device_id_type=MESH
+        )
+        return carry
+
+    lax.fori_loop(1, owners, greet, 0)
+
     col_acc[...] = jnp.full(col_acc.shape, LOW, jnp.float32)
     row_acc[...] = jnp.full(row_acc.shape, LOW, jnp.float32)
     plane_meta[0] = meta[...]
     load.wait()
-    pl.semaphore_wait(barrier, len(peers))
+    pl.semaphore_wait(barrier, owners - 1)
 
     def remote(src, dst, ssem, rsem, peer):
         return pltpu.make_async_remote_copy(
@@ -115,7 +131,7 @@
         row_key[a] = jnp.broadcast_to(source[0:1, :], (128, rows)).T
         row_cluster[a] = jnp.broadcast_to(source[1:2, :], (128, rows)).T
 
-    def pairs(a, left, d, both):
+    def pairs(a, left, d, both, t0=0, t1=None):
         right = planes[d]
         keys, clusters = plane_meta[d, 0:1, :], plane_meta[d, 1:2, :]
 
@@ -138,7 +154,7 @@
             row_acc[a, here, :] = acc
             return carry
 
-        lax.fori_loop(0, rows // TILE, step, 0)
+        lax.fori_loop(t0, rows // TILE if t1 is None else t1, step, 0)
 
     spread(0, meta)
     own = planes.at[0]
@@ -148,16 +164,23 @@
     to_plane(1).wait_recv()
     pairs(0, own, 1, False)
 
+    spread(1, z_meta.at[0])
+    spread(2, z_meta.at[1])
+
     for k in range(CHUNKS):
         @pl.when((z == 1) | (z == 2))
         def _():
             own_to_z(k, 0, -1).wait_recv()
             relay(k, 0, 1, -1).start()
 
-        @pl.when(z == 2)
-        def _():
-            own_to_z(k, 1, 2).wait_recv()
-            relay(k, 1, 0, 1).start()
+    def pass_on(ks):
+        for k in ks:
+            @pl.when(z == 2)
+            def _():
+                own_to_z(k, 1, 2).wait_recv()
+                relay(k, 1, 0, 1).start()
+
+    pass_on(range(CHUNKS // 2))
 
     def plane_step(j, carry):
         pltpu.make_async_copy(planes.at[2 * j], planes.at[2 * j], p_recv.at[2 * j]).wait()
@@ -167,32 +190,39 @@
         pairs(0, own, 2 * j + 1, False)
         return carry
 
-    lax.fori_loop(1, tiles, plane_step, 0)
-
-    for k in range(CHUNKS):
-        @pl.when((z == 0) | (z == 3))
-        def _():
-            own_to_z(k, 0, -1).wait_recv()
-
-        @pl.when(z != 2)
-        def _():
-            own_to_z(k, 1, 2).wait_recv()
-
-    spread(1, z_meta.at[0])
-    spread(2, z_meta.at[1])
-
-    def z1_step(d, carry):
-        pairs(1, zs.at[0], d, True)
-        return carry
-
-    lax.fori_loop(0, count, z1_step, 0)
+    def arrive(ks):
+        for k in ks:
+            @pl.when((z == 0) | (z == 3))
+            def _():
+                own_to_z(k, 0, -1).wait_recv()
+
+            @pl.when(z != 2)
+            def _():
+                own_to_z(k, 1, 2).wait_recv()
+
     first = lax.div(z, 2) * (count // 2)
-
-    def z2_step(d, carry):
-        pairs(2, zs.at[1], d + first, True)
-        return carry
-
-    lax.fori_loop(0, count // 2, z2_step, 0)
+    middle = rows // TILE // 2
+
+    def z_pairs(d0, d1, t0, t1):
+        def step(d, carry):
+            pairs(1, zs.at[0], d, True, t0, t1)
+
+            @pl.when((d >= first) & (d < first + count // 2))
+            def _():
+                pairs(2, zs.at[1], d, True, t0, t1)
+
+            return carry
+
+        lax.fori_loop(d0, d1, step, 0)
+
+    lax.fori_loop(1, tiles - 1, plane_step, 0)
+    arrive(range(CHUNKS // 2))
+    z_pairs(0, count - 2, 0, middle)
+    pass_on(range(CHUNKS // 2, CHUNKS))
+    plane_step(tiles - 1, 0)
+    z_pairs(count - 2, count, 0, middle)
+    arrive(range(CHUNKS // 2, CHUNKS))
+    z_pairs(0, count, middle, 2 * middle)
 
     def fold(a):
         return jnp.max(row_acc[a].T.reshape(16, 8, rows), axis=0)
@@ -213,6 +243,8 @@
     for copy in z_copies:
         copy.start()
 
+    wanted = jnp.broadcast_to(target[...], (128, rows)).T
+
     @pl.when(z >= 1)
     def _():
         for k in range(CHUNKS):
@@ -243,19 +275,54 @@
     for d in range(1, count):
         mine = jnp.maximum(mine, back[d])
     mine = jnp.maximum(mine, jnp.maximum(z_back[0], z_back[1]))
-    best[...] = jnp.maximum(jnp.max(mine, axis=0, keepdims=True), -1.0)
-
-
-def similarities(units, meta, groups, members):
+    best = jnp.maximum(jnp.max(mine, axis=0, keepdims=True), -1.0)
+    similar = jnp.broadcast_to(best, (128, rows)).T
+    lane = lax.broadcasted_iota(jnp.int32, (rows, 128), 1).astype(jnp.float32)
+    for t in range(slot_send.shape[0]):
+        hit = jnp.where(wanted == lane + float(t * 128), similar, -1.0)
+        slot_send[t] = jnp.max(hit, axis=0, keepdims=True)
+
+    def slot_copy(r):
+        o, peer = other_device(r)
+        return remote(
+            slot_send.at[lax.div(o, shared)], slot_recv.at[me], s_send.at[r], s_recv.at[me], peer
+        )
+
+    def send_slots(r, carry):
+        slot_copy(r).start()
+        return carry
+
+    def wait_slots(r, carry):
+        slot_copy(r).wait_send()
+        source = (me + r) % owners
+        pltpu.make_async_copy(
+            slot_recv.at[source], slot_recv.at[source], s_recv.at[source]
+        ).wait()
+        return carry
+
+    lax.fori_loop(1, owners, send_slots, 0)
+    slot_recv[me] = slot_send[lax.div(me, shared)]
+    lax.fori_loop(1, owners, wait_slots, 0)
+    got = slot_recv[...].reshape(owners, 128)
+    mine_at = me % shared
+    picked = got[:, :capacity]
+    for q in range(1, shared):
+        picked = jnp.where(mine_at == q, got[:, q * capacity : (q + 1) * capacity], picked)
+    out[...] = picked
+
+
+def similarities(units, meta, target, groups, members, capacity):
     rows, width = units.shape
     ys = members // NZ
     count = groups * ys
+    owners = groups * members
     dma = pltpu.SemaphoreType.DMA
     return pl.pallas_call(
-        functools.partial(kernel, groups, ys),
-        out_shape=jax.ShapeDtypeStruct((1, rows), jnp.float32),
+        functools.partial(kernel, groups, members),
+        out_shape=jax.ShapeDtypeStruct((owners, capacity), jnp.float32),
         in_specs=[
             pl.BlockSpec(memory_space=pl.ANY),
+            pl.BlockSpec(memory_space=pltpu.VMEM),
             pl.BlockSpec(memory_space=pltpu.VMEM),
         ],
         out_specs=pl.BlockSpec(memory_space=pltpu.VMEM),
@@ -271,6 +338,8 @@
             pltpu.VMEM((count, 8, rows), jnp.float32),
             pltpu.VMEM((2, 8, rows), jnp.float32),
             pltpu.VMEM((2, 8, rows), jnp.float32),
+            pltpu.VMEM((owners * capacity // 128, 1, 128), jnp.float32),
+            pltpu.VMEM((owners, 1, 128), jnp.float32),
             dma(()),
             dma((count,)), dma((count,)),
             dma((2, CHUNKS)), dma((2, CHUNKS)),
@@ -279,11 +348,12 @@
             dma((count,)), dma((count,)),
             dma((2,)), dma((2,)),
             dma((2, CHUNKS)),
+            dma((owners,)), dma((owners,)),
         ],
         compiler_params=pltpu.CompilerParams(
             collective_id=0, has_side_effects=True, vmem_limit_bytes=56 * 1024 * 1024
         ),
-    )(units, meta)
+    )(units, meta, target)
 
 
 def local(embeddings, cluster_id, row_order, assignment, placement):
@@ -299,19 +369,15 @@
         * (1.0 / math.sqrt(feature_count))
     ).astype(jnp.bfloat16)
     meta = jnp.stack([row_order, cluster_id]).astype(jnp.float32)
-    best = similarities(unit_rows, meta, groups, members)
 
     table_hits = cluster_id[:, None] == jnp.arange(assignment.shape[0], dtype=jnp.int32)[None, :]
     group_of = jnp.sum(jnp.where(table_hits, assignment[None, :], 0), axis=1)
     owner_id = group_of * members + placement
     before = jnp.arange(row_count)[None, :] < jnp.arange(row_count)[:, None]
     rank = jnp.sum((before & (owner_id[None, :] == owner_id[:, None])).astype(jnp.int32), axis=1)
-    target = owner_id * capacity + rank
-    slots = jnp.arange(owners * capacity, dtype=jnp.int32)
-    filled = jnp.max(
-        jnp.where(slots[:, None] == target[None, :], best, -1.0), axis=1
-    )
-    return lax.all_to_all(filled, ("grp", "mem"), split_axis=0, concat_axis=0, tiled=True)
+    target = (owner_id * capacity + rank).astype(jnp.float32)[None, :]
+    filled = similarities(unit_rows, meta, target, groups, members, capacity)
+    return filled.reshape(owners * capacity)
 
 
 def solution(mesh):

time: 80.5 us -> 85.2 us (1.058)
  Pallas kernels: 63.8 us -> 77.9 us
  blocking collectives: 9.99 us -> 0 us
    pallas_call x1, Pallas kernels: 63.8 us -> 77.9 us  [similarities(): pl.pallas_call(functools.partial(kernel, groups, members), out_shape=jax....]
    all_to_all x1 -> x0, blocking collectives: 9.99 us -> none  [local(): lax.all_to_all(filled, ('grp', 'mem'), split_axis=0, concat_axis=0, tiled...]
    reshape x0 -> x1, local copies, waits for them, and re-layouts: none -> 1.38 us  [local(): return filled.reshape(owners * capacity)]
    all_to_all x3 -> x0, local copies, waits for them, and re-layouts: 1.25 us -> none  [local(): lax.all_to_all(filled, ('grp', 'mem'), split_axis=0, concat_axis=0, tiled...]
    reduce_max x1 -> x0, other arithmetic: 0.97 us -> none  [local(): jnp.max(jnp.where(slots[:, None] == target[None, :], best, -1.0), axis=1)]
where the time goes in v3:
time: 85.2 us; the launch traced here: 84.9 us
  Pallas kernels  77.9 us (91%)
  other arithmetic  5.5 us (6%)
  local copies, waits for them, and re-layouts  1.39 us (2%)
    pallas_call x1, Pallas kernels, similarities(): pl.pallas_call(functools.partial(kernel, groups, members), out_shape=jax....  77.9 us

profile of v3, /device:TPU:0, one launch (start us, length us, event | category | flops | bytes accessed | tf_op | source)
XLA Modules:
  0.0 84.9 jit_solution(3051903205881486239)
XLA Ops:
  0.0 0.0 copy-start.1
  0.0 0.0 copy-start
  0.0 0.0 copy-start.2
  0.0 0.9 %select_reduce_fusion = s32[512]{0:T(512)S(1)} fusion(s32[4]{0:T(128)} %param.8, s32[512]{0:T(512)} %param.6), kind=kLoop, calls=%fused_computation.8 | loop fusion | flops 5632 | bytes 4112 | tf_op jit(solution)/shard_map/reduce_sum | solution.py:374
  0.9 0.7 multiply_add_fusion
  1.6 0.3 convert_reduce_fusion
  1.8 0.6 add_convert_fusion.1
  2.4 1.4 %fusion = f32[512]{0:T(512)S(1)} fusion(bf16[512,768]{1,0:T(8,128)(2,1)} %param.5), kind=kLoop, calls=%fused_computation.2 | loop fusion | flops 1179136 | bytes 788480 | tf_op jit(solution)/shard_map/reduce_sum | solution.py:368
  3.8 0.0 copy-done.1
  3.8 0.0 copy-done.2
  3.8 0.6 add_convert_fusion.meta
  4.4 0.0 copy-done
  4.4 1.1 %fusion.2.units = bf16[512,768]{1,0:T(8,128)(2,1)} fusion(bf16[512,768]{1,0:T(8,128)(2,1)S(1)} %copy-done, f32[512]{0:T(512)S(1)} %add_rsqrt_fusion), kind=kLoop, calls=%fused_computation.4 | loop fusion | flops 1572864 | bytes 1574912 | tf_op jit(solution)/shard_map/convert_element_type | solution.py:370
  5.5 77.9 %shard_map.55 = f32[32,32]{1,0:T(8,128)} custom-call(bf16[512,768]{1,0:T(8,128)(2,1)} %fusion.2.units, f32[2,512]{1,0:T(2,128)} %add_convert_fusion.meta, f32[1,512]{1,0:T(1,128)} %bitcast.3), custom_call_target="tpu_custom_call" | custom-call | tf_op jit(solution)/shard_map/pallas_call | solution.py:320
  83.5 1.4 %reshape.15 = f32[1024]{0:T(1024)} reshape(f32[32,32]{1,0:T(8,128)} %shard_map.55) | data formatting | bytes 8192 | tf_op jit(solution)/shard_map/reshape | solution.py:380
  (1 shorter events, 0.0 us)
Async XLA Ops:
  0.0 3.8 %copy-start.1 = (s32[512]{0:T(512)S(1)}, s32[512]{0:T(512)}, u32[]{:S(2)}) copy-start(s32[512]{0:T(512)} %param.6) | copy-start | bytes 6148
  0.0 4.4 %copy-start = (bf16[512,768]{1,0:T(8,128)(2,1)S(1)}, bf16[512,768]{1,0:T(8,128)(2,1)}, u32[]{:S(2)}) copy-start(bf16[512,768]{1,0:T(8,128)(2,1)} %param.5) | copy-start | bytes 2359300
  0.0 3.8 %copy-start.2 = (s32[512]{0:T(512)S(1)}, s32[512]{0:T(512)}, u32[]{:S(2)}) copy-start(s32[512]{0:T(512)} %param.7) | copy-start | bytes 6148
